TPU v7x, 32 devices: a whole 2x2x4 slice. The times are simulated.
32 devices in a mesh: seg: 8 (over z, core), bond: 4 (over y, x).
Axes of the slice: x: 2, y: 2, z: 4, core: 2. Of those that a mesh axis runs over, the one named last changes fastest.
Arguments:
- left_env: bfloat16 [8, 1024, 6, 1024], P('seg', 'bond'), may hold values from -0.1875 to 0.1875
- prev_left: bfloat16 [8, 1024, 1024], P('seg'), may hold values from -0.25 to 1.25
- cur_site: bfloat16 [8, 1024, 4, 1024], P('seg', 'bond'), may hold values from -6 to 6
- prev_site: bfloat16 [8, 1024, 4, 1024], P('seg', None, None, 'bond'), may hold values from -6 to 6
- hamiltonian: bfloat16 [8, 6, 6, 4, 4], P('seg'), may hold values from -1.25 to 1.25
- right_env: bfloat16 [8, 1024, 6, 1024], P('seg', 'bond'), may hold values from -0.078125 to 0.078125
- prev_right: bfloat16 [8, 1024, 1024], P('seg'), may hold values from -0.25 to 1.25
Outputs:
- new_site: bfloat16 [8, 1024, 4, 1024], P('seg', 'bond')
- center: float32 [8, 1024, 1024], P('seg', 'bond')
All inputs are finite; a program needn't handle non-finite values.
Results may differ from a plain program's by a relative error of at most 0.0054.
Values may be sent and summed in bfloat16 or wider, within the bound.
A program may use at most 128 MiB of HBM per device.

v0:
```python
import math

import jax
import jax.numpy as jnp
from jax import lax
from jax.sharding import PartitionSpec as P

PHYS = 4
MPOB = 6


def shifted(block, axis, distance):
    devices = range(lax.axis_size(axis))
    route = [((i - distance) % len(devices), i) for i in devices]
    return lax.ppermute(block, axis, route)


def shards(left_env, prev_left, cur_site, prev_site, hamiltonian, right_env, prev_right):
    left_now, prev_now = shifted((left_env[0], prev_left[0]), "seg", 1)
    own_rows = left_now.shape[0]
    bond_width = left_now.shape[2]
    coupling = hamiltonian[0].astype(jnp.float32)
    current = lax.all_gather(cur_site[0], "bond", axis=0, tiled=True)
    projected = jnp.dot(
        left_now.reshape(own_rows * MPOB, bond_width),
        current.reshape(bond_width, PHYS * bond_width),
        preferred_element_type=jnp.float32,
    ).reshape(own_rows, MPOB, PHYS, bond_width)
    mixture = jnp.einsum(
        "autc,uvst->asvc", projected, coupling, precision=lax.Precision.HIGHEST
    ).astype(jnp.bfloat16)
    applied = jnp.einsum(
        "asvc,cvy->asy",
        mixture,
        lax.all_gather(right_env[0], "bond", axis=0, tiled=True),
        preferred_element_type=jnp.float32,
    )
    partial_value = jnp.einsum(
        "ab,bsc->asc", prev_now, prev_site[0], preferred_element_type=jnp.float32
    ).astype(jnp.bfloat16)
    second = jnp.einsum(
        "akc,cy->aky",
        lax.all_to_all(partial_value, "bond", split_axis=0, concat_axis=2, tiled=True),
        prev_right[0],
        preferred_element_type=jnp.float32,
    )
    target = (2.0 * applied - second).reshape(own_rows * PHYS, bond_width)
    local_correlation = jnp.dot(
        target.T, target, precision=lax.Precision.HIGHEST, preferred_element_type=jnp.float32
    )
    correlation = lax.psum(local_correlation, "bond")
    triangle = jnp.linalg.cholesky(correlation)
    solved = jax.scipy.linalg.solve_triangular(triangle, target.T, lower=True)
    norming = math.sqrt(bond_width * PHYS)
    new_site = (solved.T * norming).astype(jnp.bfloat16).reshape(1, own_rows, PHYS, bond_width)
    offset = lax.axis_index("bond") * own_rows
    center = lax.dynamic_slice_in_dim(triangle.T, offset, own_rows, 0) / norming
    return (new_site, center[None])


def solution(mesh):
    return jax.shard_map(
        shards,
        mesh=mesh,
        in_specs=(
            P("seg", "bond", None, None),
            P("seg", None, None),
            P("seg", "bond", None, None),
            P("seg", None, None, "bond"),
            P("seg", None, None, None, None),
            P("seg", "bond", None, None),
            P("seg", None, None),
        ),
        out_specs=(P("seg", "bond", None, None), P("seg", "bond", None)),
        check_vma=False,
    )
```

profile of v0, /device:TPU:0, one launch (start us, length us, event | category | flops | bytes accessed | tf_op | source)
XLA Modules:
  0.0 759.1 jit_solution(3926485406650583413)
XLA Ops:
  11.9 25.3 %collective-permute-done.1 = bf16[1024,1024]{1,0:T(8,128)(2,1)S(1)} collective-permute-done((bf16[1024,1024]{1,0:T(8,128)(2,1)}, bf16[1024,1024]{1,0:T(8,128)(2,1)S(1)}, u32[]{:S(2)}, u32[]{:S(2)}) %collective-permute-start.1) | collective-permute-done | bytes 2097184 | tf_op jit(solution)/shard_map/ppermute | solution.py:15
  41.2 40.1 %all_to_all.18 = bf16[1024,4,256]{2,1,0:T(4,128)(2,1)S(1)} all-to-all(bf16[1024,4,256]{2,1,0:T(4,128)(2,1)S(1)} %copy.30), channel_id=1, replica_groups=mesh['seg'=8,'bond'=4] {'bond'}, dimensions={0} | all-to-all | bytes 4194304 | tf_op jit(solution)/shard_map/all_to_all | solution.py:43
  92.1 22.9 %all-gather.5.cloned.1.call-done = bf16[1,1024,4,1024]{3,2,0,1:T(4,128)(2,1)} async-done(((bf16[1,256,4,1024]{3,2,0,1:T(4,128)(2,1)}), bf16[1,1024,4,1024]{3,2,0,1:T(4,128)(2,1)}) %all-gather.5.cloned.1.call-update) | async-done | bytes 8388624 | tf_op jit(solution)/shard_map/all_gather | solution.py:23
  115.0 14.1 %copy.45 = bf16[1,1024,4,1024]{1,3,2,0:T(8,128)(2,1)} copy(bf16[1,1024,4,1024]{3,2,0,1:T(4,128)(2,1)} %all-gather.5.cloned.1.call-done) | data formatting | bytes 16777216 | tf_op jit(solution)/shard_map/reshape | solution.py:26
  129.1 21.9 %convolution_bitcast_fusion = f32[256,6,4,1024,1]{3,0,2,1,4:T(8,128)} fusion(bf16[1,1024,4,1024]{1,3,2,0:T(8,128)(2,1)} %copy.45, bf16[256,6,1024]{2,0,1:T(8,128)(2,1)} %collective-permute-done), kind=kOutput, calls=%fused_computation.9 | convolution fusion | flops 12884901888 | bytes 36700160 | tf_op jit(solution)/shard_map/dot_general | solution.py:24
  151.0 62.8 %fusion.2 = bf16[256,4,6,1024]{3,2,1,0:T(8,128)(2,1)} fusion(f32[256,6,4,1024,1]{3,0,2,1,4:T(8,128)} %convolution_bitcast_fusion, bf16[1,6,6,4,4]{2,4,3,1,0:T(4,128)(2,1)S(1)} %copy-done.5), kind=kOutput, calls=%fused_computation.5 | convolution fusion | flops 1818230784 | bytes 37749888 | tf_op jit(solution)/shard_map/autc,uvst->asvc/dot_general | solution.py:29
  213.7 25.5 %all-gather.7.cloned.1.call-done = bf16[1,1024,6,1024]{3,1,2,0:T(8,128)(2,1)} async-done(((bf16[1,256,6,1024]{3,1,2,0:T(8,128)(2,1)}), bf16[1,1024,6,1024]{3,1,2,0:T(8,128)(2,1)}) %all-gather.7.cloned.1.call-update) | async-done | bytes 12582928 | tf_op jit(solution)/shard_map/all_gather | solution.py:35
  239.2 32.4 %fusion.10 = f32[256,4,1024]{2,0,1:T(8,128)S(1)} fusion(f32[256,4,1024]{2,0,1:T(8,128)} %fusion.26, bf16[1,1024,6,1024]{3,1,2,0:T(8,128)(2,1)} %all-gather.7.cloned.1.call-done, bf16[256,4,6,1024]{3,2,1,0:T(8,128)(2,1)} %fusion.2), kind=kOutput, calls=%fused_computation.14 | convolution fusion | flops 12886999040 | bytes 33554432 | tf_op jit(solution)/shard_map/asvc,cvy->asy/dot_general | solution.py:32
  273.6 15.1 %convolution_bitcast_fusion.1 = f32[1024,1024]{0,1:T(8,128)} fusion(f32[256,4,1024]{2,0,1:T(8,128)S(1)} %fusion.10), kind=kOutput, calls=%fused_computation.20 | convolution fusion | flops 12884901888 | bytes 8388608 | tf_op jit(solution)/shard_map/dot_general | solution.py:48
  306.4 86.1 %all-reduce.3.cloned.1.call-done = f32[1024,1024]{0,1:T(8,128)} async-done(((f32[1024,1024]{0,1:T(8,128)}), f32[1024,1024]{0,1:T(8,128)}) %all-reduce.3.cloned.1.call-update) | async-done | bytes 4194320 | tf_op jit(solution)/shard_map/psum | solution.py:51
  404.7 11.7 %cholesky.223 = f32[128,128]{1,0:T(8,128)S(1)} custom-call(f32[128,128]{1,0:T(8,128)S(1)} %cholesky.580), custom_call_target="Cholesky" | custom-call | tf_op jit(solution)/shard_map/jit(cholesky)/cholesky | solution.py:52
  416.4 9.8 %custom-call.63 = f32[1,128,128]{1,2,0:T(8,128)S(1)} custom-call(f32[1,128,128]{2,1,0:T(8,128)S(1)} %get-tuple-element.74), custom_call_target="InvertDiagBlocksLowerTriangular" | custom-call | tf_op jit(solution)/shard_map/jit(cholesky)/cholesky | solution.py:52
  432.7 11.9 %cholesky.244 = f32[128,128]{1,0:T(8,128)S(1)} custom-call(f32[128,128]{1,0:T(8,128)S(1)} %cholesky.584), custom_call_target="Cholesky" | custom-call | tf_op jit(solution)/shard_map/jit(cholesky)/cholesky | solution.py:52
  445.2 9.8 %custom-call.64 = f32[1,128,128]{1,2,0:T(8,128)S(1)} custom-call(f32[1,128,128]{2,1,0:T(8,128)S(1)} %get-tuple-element.71), custom_call_target="InvertDiagBlocksLowerTriangular" | custom-call | tf_op jit(solution)/shard_map/jit(cholesky)/cholesky | solution.py:52
  458.4 11.7 %cholesky.468 = f32[128,128]{1,0:T(8,128)S(1)} custom-call(f32[128,128]{1,0:T(8,128)S(1)} %cholesky.589), custom_call_target="Cholesky" | custom-call | tf_op jit(solution)/shard_map/jit(cholesky)/cholesky | solution.py:52
  484.7 11.9 %cholesky.487 = f32[128,128]{1,0:T(8,128)S(1)} custom-call(f32[128,128]{1,0:T(8,128)S(1)} %cholesky.594), custom_call_target="Cholesky" | custom-call | tf_op jit(solution)/shard_map/jit(cholesky)/cholesky | solution.py:52
  511.2 11.7 %cholesky.506 = f32[128,128]{1,0:T(8,128)S(1)} custom-call(f32[128,128]{1,0:T(8,128)S(1)} %cholesky.599), custom_call_target="Cholesky" | custom-call | tf_op jit(solution)/shard_map/jit(cholesky)/cholesky | solution.py:52
  524.2 10.2 %custom-call.67 = f32[1,128,128]{1,2,0:T(8,128)S(1)} custom-call(f32[1,128,128]{2,1,0:T(8,128)S(1)} %get-tuple-element.62), custom_call_target="InvertDiagBlocksLowerTriangular" | custom-call | tf_op jit(solution)/shard_map/jit(cholesky)/cholesky | solution.py:52
  537.7 11.7 %cholesky.526 = f32[128,128]{1,0:T(8,128)S(1)} custom-call(f32[128,128]{1,0:T(8,128)S(1)} %cholesky.604), custom_call_target="Cholesky" | custom-call | tf_op jit(solution)/shard_map/jit(cholesky)/cholesky | solution.py:52
  563.5 11.9 %cholesky.546 = f32[128,128]{1,0:T(8,128)S(1)} custom-call(f32[128,128]{1,0:T(8,128)S(1)} %cholesky.609), custom_call_target="Cholesky" | custom-call | tf_op jit(solution)/shard_map/jit(cholesky)/cholesky | solution.py:52
  576.6 9.8 %custom-call.69 = f32[1,128,128]{1,2,0:T(8,128)S(1)} custom-call(f32[1,128,128]{2,1,0:T(8,128)S(1)} %get-tuple-element.56), custom_call_target="InvertDiagBlocksLowerTriangular" | custom-call | tf_op jit(solution)/shard_map/jit(cholesky)/cholesky | solution.py:52
  589.0 11.7 %cholesky.564 = f32[128,128]{1,0:T(8,128)S(1)} custom-call(f32[128,128]{1,0:T(8,128)S(1)} %convolution_subtract_fusion.11), custom_call_target="Cholesky" | custom-call | tf_op jit(solution)/shard_map/jit(cholesky)/cholesky | solution.py:52
  614.3 23.0 %while.1 = (s32[]{:T(128)}, f32[1024,1024]{1,0:T(8,128)}, s32[8,2]{0,1:T(2,128)S(1)}, f32[8,128,128]{2,1,0:T(8,128)S(1)}, s32[]{:T(128)}) while((s32[]{:T(128)}, f32[1024,1024]{1,0:T(8,128)}, s32[8,2]{0,1:T(2,128)S(1)}, f32[8,128,128]{2,1,0:T(8,128)S(1)}, s32[]{:T(128)}) %tuple.65), condition=%wide.while_cond, body=%wide.while_body.sunk | while | flops 2 | bytes 131181 | solution.py:53
  637.3 78.8 %custom-call.70 = f32[8,128,128]{1,2,0:T(8,128)S(1)} custom-call(f32[8,128,128]{2,1,0:T(8,128)S(1)} %get-tuple-element.9), custom_call_target="InvertDiagBlocksLowerTriangular" | custom-call | tf_op jit(solution)/shard_map/jit(_solve_triangular)/triangular_solve | solution.py:53
  (119 shorter events, 180.9 us)
Async XLA Ops:
  7.2 30.0 %copy-start = (bf16[1,1024,4,256]{3,2,1,0:T(4,128)(2,1)S(1)}, bf16[1,1024,4,256]{3,2,1,0:T(4,128)(2,1)}, u32[]{:S(2)}) copy-start(bf16[1,1024,4,256]{3,2,1,0:T(4,128)(2,1)} %param.10) | copy-start | bytes 6291460
  7.2 107.8 %all-gather.5.cloned.1.call-start = ((), (), s32[]{:S(2)}) async-start(), calls=%async_computation.2 | async-start | bytes 10485760 | tf_op jit(solution)/shard_map/all_gather | solution.py:23
  7.9 231.3 %all-gather.7.cloned.1.call-start = ((), (), s32[]{:S(2)}) async-start(), calls=%async_computation.3 | async-start | bytes 15728640 | tf_op jit(solution)/shard_map/all_gather | solution.py:35
  8.7 383.9 %all-reduce.3.cloned.1.call-start = ((), (), s32[]{:S(2)}) async-start(), calls=%async_computation.1 | async-start | bytes 8388608 | tf_op jit(solution)/shard_map/psum | solution.py:51
  8.7 28.5 %collective-permute-start.1 = (bf16[1024,1024]{1,0:T(8,128)(2,1)}, bf16[1024,1024]{1,0:T(8,128)(2,1)S(1)}, u32[]{:S(2)}, u32[]{:S(2)}) collective-permute-start(bf16[1024,1024]{1,0:T(8,128)(2,1)} %bitcast.186), channel_id=1, source_target_pairs={{28,0},{0,4},{4,8},{8,12},{12,16},{16,20},{20,24},{24,28},{29,1},{... | collective-permute-start | bytes 6291464 | tf_op jit(solution)/shard_map/ppermute | solution.py:15
  9.3 119.9 %collective-permute-start = (bf16[256,6,1024]{2,0,1:T(8,128)(2,1)}, bf16[256,6,1024]{2,0,1:T(8,128)(2,1)}, u32[]{:S(2)}, u32[]{:S(2)}) collective-permute-start(bf16[256,6,1024]{2,0,1:T(8,128)(2,1)} %bitcast.185), channel_id=1, source_target_pairs={{28,0},{0,4},{4,8},{8,12},{12,16},{16,20},{20,24},{24,28},{29,1},{... | collective-permute-start | bytes 9437192 | tf_op jit(solution)/shard_map/ppermute | solution.py:15
  129.1 21.9 %copy-start.5 = (bf16[1,6,6,4,4]{2,4,3,1,0:T(4,128)(2,1)S(1)}, bf16[1,6,6,4,4]{2,4,3,1,0:T(4,128)(2,1)}, u32[]{:S(2)}) copy-start(bf16[1,6,6,4,4]{2,4,3,1,0:T(4,128)(2,1)} %param.11) | copy-start | bytes 3460
  271.7 1.9 copy-start.4
  402.7 2.0 copy-start.3
  716.2 4.3 copy-start.2
  741.5 10.8 %copy-start.1 = (bf16[1,1024,4,256]{3,2,1,0:T(4,128)(2,1)S(1)}, bf16[1,1024,4,256]{3,2,1,0:T(4,128)(2,1)}, u32[]{:S(2)}) copy-start(bf16[1,1024,4,256]{3,2,1,0:T(4,128)(2,1)} %param.10) | copy-start | bytes 6291460
Sparse Core Ops, SparseCore 0:
  9.8 105.0 all-gather.4
  116.8 122.3 all-gather.6
  288.9 103.5 all-reduce.2
where the time goes:
time: 764 us; the launch traced here: 759 us
  other arithmetic  265 us (35%)
  matrix products  187 us (24%)
  waiting for transfers between devices  161 us (21%)
  local copies, waits for them, and re-layouts  82.3 us (11%)
  blocking collectives  40.1 us (5%)
  between operations  19.3 us (3%)
    another operation x30, other arithmetic, shards(): triangle = jnp.linalg.cholesky(correlation)  172 us
    psum x1, waiting for transfers between devices, shards(): correlation = lax.psum(local_correlation, 'bond')  86.1 us
    another operation x3, other arithmetic, shards(): solved = jax.scipy.linalg.solve_triangular(triangle, target.T, lower=True)  85.5 us
    dot_general x1, matrix products, shards(): jnp.einsum('autc,uvst->asvc', projected, coupling, precision=lax.Precisio...  62.8 us
    all_to_all x1, blocking collectives, shards(): lax.all_to_all(partial_value, 'bond', split_axis=0, concat_axis=2, tiled=...  40.1 us
    dot_general x1, matrix products, shards(): jnp.einsum('asvc,cvy->asy', mixture, lax.all_gather(right_env[0], 'bond',...  32.4 us
    all_gather x1, waiting for transfers between devices, shards(): lax.all_gather(right_env[0], 'bond', axis=0, tiled=True)  25.5 us
    ppermute x2, waiting for transfers between devices, shifted(): return lax.ppermute(block, axis, route)  25.3 us
  transfers between devices with their start and end apart: 5, of which 4 were waited for; matrix products, arithmetic and copies ran while one was open for 17% of the time, Pallas kernels for 0%

commit v1 on v0

--- a/solution.py
+++ b/solution.py
@@ -3,16 +3,130 @@
 import jax
 import jax.numpy as jnp
 from jax import lax
+from jax.experimental import pallas as pl
+from jax.experimental.pallas import tpu as pltpu
 from jax.sharding import PartitionSpec as P
 
 PHYS = 4
 MPOB = 6
+BLOCK = 128
+STRIP = 256
+GROUP = 4
 
 
 def shifted(block, axis, distance):
     devices = range(lax.axis_size(axis))
     route = [((i - distance) % len(devices), i) for i in devices]
     return lax.ppermute(block, axis, route)
+
+
+def halves(x):
+    high = x.astype(jnp.bfloat16)
+    return high, (x - high.astype(jnp.float32)).astype(jnp.bfloat16)
+
+
+def product(a, b, dims):
+    a_high, a_low = halves(a)
+    b_high, b_low = halves(b)
+
+    def dot(x, y):
+        return lax.dot_general(x, y, (dims, ((), ())), preferred_element_type=jnp.float32)
+
+    return dot(a_high, b_high) + (dot(a_high, b_low) + dot(a_low, b_high))
+
+
+def eliminate(block, rows_ref):
+    size = block.shape[0]
+    lane = lax.broadcasted_iota(jnp.int32, (1, size), 1)
+    rest = block
+    top = 0
+    for first in range(0, size, GROUP):
+        start = first // 8 * 8
+        rest, top = rest[start - top :], start
+        at = first - top
+        rows = [rest[at + q : at + q + 1, :] for q in range(GROUP)]
+        columns = [
+            jnp.broadcast_to(rest[:, first + q : first + q + 1], rest.shape) for q in range(GROUP)
+        ]
+        small = [[columns[r][at + p : at + p + 1, :] for r in range(GROUP)] for p in range(GROUP)]
+        change = None
+        for q in range(GROUP):
+            rows_ref[pl.ds(first + q, 1), :] = rows[q]
+            inverse = 1.0 / small[q][q]
+            lead = jnp.where(lane == first + q, 1.0, rows[q])
+            for p in range(q + 1, GROUP):
+                factor = small[q][p] * inverse
+                for r in range(p, GROUP):
+                    small[p][r] = small[p][r] - factor * small[q][r]
+                rows[p] = jnp.where(lane == first + q, 0.0, rows[p]) - factor * lead
+                columns[p] = columns[p] - factor * columns[q]
+            if first + GROUP < size:
+                lead = jnp.where((lane > first + q) & (lane < first + GROUP), 0.0, lead)
+                term = columns[q] * (inverse * lead)
+                change = term if change is None else change + term
+        if first + GROUP < size:
+            rest = jnp.where((lane >= first) & (lane < first + GROUP), 0.0, rest) - change
+
+
+def factor_kernel(packed_ref, upper_ref, inverse_ref, work, panel, rows_ref):
+    size = work.shape[0]
+    blocks = size // BLOCK
+    offset = 0
+    for start in range(0, size, STRIP):
+        width = size - start
+        work[start : start + STRIP, start:] = packed_ref[:, offset : offset + width]
+        if start > 0:
+            work[start : start + STRIP, :start] = jnp.zeros((STRIP, start), jnp.float32)
+        offset += width
+    row = lax.broadcasted_iota(jnp.int32, (BLOCK, BLOCK), 0)
+    column = lax.broadcasted_iota(jnp.int32, (BLOCK, BLOCK), 1)
+    full_column = lax.broadcasted_iota(jnp.int32, (BLOCK, size), 1)
+
+    def step(k, carry):
+        own = pl.ds(pl.multiple_of(k * BLOCK, BLOCK), BLOCK)
+        eliminate(work[own, own], rows_ref)
+        done = rows_ref[...]
+        pivots = jnp.sum(jnp.where(row == column, done, 0.0), axis=1, keepdims=True)
+        scale = lax.rsqrt(pivots)
+        scaled = done * scale
+        upper = jnp.where(row <= column, scaled, 0.0)
+        inverse = jnp.where(row > column, scaled, jnp.where(row == column, scale, 0.0))
+        panel[...] = product(inverse, work[own, :], ((1,), (0,)))
+        whole = panel[...]
+        upper_ref[own, :] = jnp.where(full_column >= (k + 1) * BLOCK, whole, 0.0)
+        inverse_ref[own, :] = jnp.where(full_column < k * BLOCK, whole, 0.0)
+        upper_ref[own, own] = upper
+        inverse_ref[own, own] = inverse
+        panel[:, own] = inverse
+        right = panel[...]
+
+        def update(i, carry):
+            other = pl.ds(pl.multiple_of(i * BLOCK, BLOCK), BLOCK)
+            work[other, own] = jnp.zeros((BLOCK, BLOCK), jnp.float32)
+            work[other, :] -= product(panel[:, other], right, ((0,), (0,)))
+            return carry
+
+        lax.fori_loop(k + 1, blocks, update, 0)
+        return carry
+
+    lax.fori_loop(0, blocks, step, 0)
+
+
+def factorize(packed, size):
+    whole = jax.ShapeDtypeStruct((size, size), jnp.float32)
+    return pl.pallas_call(
+        factor_kernel,
+        out_shape=(whole, whole),
+        in_specs=[pl.BlockSpec(memory_space=pltpu.VMEM)],
+        out_specs=[pl.BlockSpec(memory_space=pltpu.VMEM)] * 2,
+        scratch_shapes=[
+            pltpu.VMEM((size, size), jnp.float32),
+            pltpu.VMEM((BLOCK, size), jnp.float32),
+            pltpu.VMEM((BLOCK, BLOCK), jnp.float32),
+        ],
+        compiler_params=pltpu.CompilerParams(vmem_limit_bytes=40 * 2**20),
+        name="factorize",
+    )(packed)
 
 
 def shards(left_env, prev_left, cur_site, prev_site, hamiltonian, right_env, prev_right):
@@ -27,7 +141,7 @@
         preferred_element_type=jnp.float32,
     ).reshape(own_rows, MPOB, PHYS, bond_width)
     mixture = jnp.einsum(
-        "autc,uvst->asvc", projected, coupling, precision=lax.Precision.HIGHEST
+        "autc,uvst->asvc", projected, coupling, precision=lax.Precision.HIGH
     ).astype(jnp.bfloat16)
     applied = jnp.einsum(
         "asvc,cvy->asy",
@@ -45,16 +159,28 @@
         preferred_element_type=jnp.float32,
     )
     target = (2.0 * applied - second).reshape(own_rows * PHYS, bond_width)
-    local_correlation = jnp.dot(
-        target.T, target, precision=lax.Precision.HIGHEST, preferred_element_type=jnp.float32
-    )
-    correlation = lax.psum(local_correlation, "bond")
-    triangle = jnp.linalg.cholesky(correlation)
-    solved = jax.scipy.linalg.solve_triangular(triangle, target.T, lower=True)
+    strips = [
+        jnp.dot(
+            target[:, start : start + STRIP].T,
+            target[:, start:],
+            precision=lax.Precision.HIGH,
+            preferred_element_type=jnp.float32,
+        )
+        for start in range(0, bond_width, STRIP)
+    ]
+    packed = lax.psum(jnp.concatenate(strips, axis=1), "bond")
+    upper, inverse = factorize(packed, bond_width)
     norming = math.sqrt(bond_width * PHYS)
-    new_site = (solved.T * norming).astype(jnp.bfloat16).reshape(1, own_rows, PHYS, bond_width)
+    solved = lax.dot_general(
+        target,
+        inverse,
+        (((1,), (1,)), ((), ())),
+        precision=lax.Precision.HIGH,
+        preferred_element_type=jnp.float32,
+    )
+    new_site = (solved * norming).astype(jnp.bfloat16).reshape(1, own_rows, PHYS, bond_width)
     offset = lax.axis_index("bond") * own_rows
-    center = lax.dynamic_slice_in_dim(triangle.T, offset, own_rows, 0) / norming
+    center = lax.dynamic_slice_in_dim(upper, offset, own_rows, 0) / norming
     return (new_site, center[None])
 
 

time: 764 us -> 451 us (0.59)
  other arithmetic: 265 us -> 4.14 us
  matrix products: 187 us -> 136 us
  Pallas kernels: 0 us -> 49.8 us
  local copies, waits for them, and re-layouts: 82.3 us -> 38.3 us
    another operation x33 -> x0, other arithmetic: 258 us -> none  [the longest x30 172 us: shards(): triangle = jnp.linalg.cholesky(correlation)]
    pallas_call x0 -> x1, Pallas kernels: none -> 49.8 us  [factorize(): pl.pallas_call(factor_kernel, out_shape=(whole, whole), in_specs=[pl.Bloc...]
    another operation x29 -> x0, matrix products: 46.4 us -> none  [the longest x15 23.3 us: shards(): solved = jax.scipy.linalg.solve_triangular(triangle, target.T, lower=True)]
    another operation x33 -> x0, local copies, waits for them, and re-layouts: 25.4 us -> none
    dot_general x1, matrix products: 62.8 us -> 54.5 us  [shards(): jnp.einsum('autc,uvst->asvc', projected, coupling, precision=lax.Precisio...]
    all_gather x1, waiting for transfers between devices: 25.5 us -> 33.7 us  [shards(): lax.all_gather(right_env[0], 'bond', axis=0, tiled=True)]
    psum x1, waiting for transfers between devices: 86.1 us -> 78.4 us  [shards(): packed = lax.psum(jnp.concatenate(strips, axis=1), 'bond')]
    dot_general x1 -> x5, matrix products: 15.1 us -> 18.4 us  [the longest x1 9.89 us: shards(): lax.dot_general(target, inverse, (((1,), (1,)), ((), ())), precision=lax....]
  transfers between devices with their start and end apart: 5 -> 5, of which waited for: 4 -> 4; matrix products, arithmetic and copies ran while one was open for 17% -> 23% of each run, Pallas kernels for 0% -> 0%
where the time goes in v1:
time: 451 us; the launch traced here: 447 us
  waiting for transfers between devices  161 us (36%)
  matrix products  136 us (30%)
  Pallas kernels  49.8 us (11%)
  blocking collectives  41.1 us (9%)
  local copies, waits for them, and re-layouts  38.3 us (8%)
  between operations  14.1 us (3%)
    psum x1, waiting for transfers between devices, shards(): packed = lax.psum(jnp.concatenate(strips, axis=1), 'bond')  78.4 us
    dot_general x1, matrix products, shards(): jnp.einsum('autc,uvst->asvc', projected, coupling, precision=lax.Precisio...  54.5 us
    pallas_call x1, Pallas kernels, factorize(): pl.pallas_call(factor_kernel, out_shape=(whole, whole), in_specs=[pl.Bloc...  49.8 us
    all_to_all x1, blocking collectives, shards(): lax.all_to_all(partial_value, 'bond', split_axis=0, concat_axis=2, tiled=...  41.1 us
    all_gather x1, waiting for transfers between devices, shards(): lax.all_gather(right_env[0], 'bond', axis=0, tiled=True)  33.7 us
    dot_general x1, matrix products, shards(): jnp.einsum('asvc,cvy->asy', mixture, lax.all_gather(right_env[0], 'bond',...  32.4 us
    ppermute x2, waiting for transfers between devices, shifted(): return lax.ppermute(block, axis, route)  25.3 us
    dot_general x1, matrix products, shards(): jnp.dot(left_now.reshape(own_rows * MPOB, bond_width), current.reshape(bo...  21.9 us
  transfers between devices with their start and end apart: 5, of which 4 were waited for; matrix products, arithmetic and copies ran while one was open for 23% of the time, Pallas kernels for 0%

profile of v1, /device:TPU:0, one launch (start us, length us, event | category | flops | bytes accessed | tf_op | source)
XLA Modules:
  0.0 447.4 jit_solution(18445857204524279054)
XLA Ops:
  9.3 2.7 collective-permute-start
  11.9 25.3 %collective-permute-done.1 = bf16[1024,1024]{1,0:T(8,128)(2,1)S(1)} collective-permute-done((bf16[1024,1024]{1,0:T(8,128)(2,1)}, bf16[1024,1024]{1,0:T(8,128)(2,1)S(1)}, u32[]{:S(2)}, u32[]{:S(2)}) %collective-permute-start.1) | collective-permute-done | bytes 2097184 | tf_op jit(solution)/shard_map/ppermute | solution.py:20
  37.2 2.3 fusion.24
  41.2 41.1 %all_to_all.18 = bf16[1024,4,256]{2,1,0:T(4,128)(2,1)S(1)} all-to-all(bf16[1024,4,256]{2,1,0:T(4,128)(2,1)S(1)} %copy.22), channel_id=1, replica_groups=mesh['seg'=8,'bond'=4] {'bond'}, dimensions={0} | all-to-all | bytes 4194304 | tf_op jit(solution)/shard_map/all_to_all | solution.py:157
  83.9 2.7 all_to_all.16
  86.6 6.5 %fusion.19 = f32[256,4,1024]{2,0,1:T(8,128)} fusion(bf16[256,4,1024]{2,0,1:T(8,128)(2,1)} %all_to_all.16, bf16[1,1024,1024]{2,1,0:T(8,128)(2,1)} %param.13), kind=kOutput, calls=%fused_computation.18 | convolution fusion | flops 2147483648 | bytes 8388608 | tf_op jit(solution)/shard_map/akc,cy->aky/dot_general | solution.py:155
  93.1 21.9 %all-gather.5.cloned.1.call-done = bf16[1,1024,4,1024]{3,2,0,1:T(4,128)(2,1)} async-done(((bf16[1,256,4,1024]{3,2,0,1:T(4,128)(2,1)}), bf16[1,1024,4,1024]{3,2,0,1:T(4,128)(2,1)}) %all-gather.5.cloned.1.call-update) | async-done | bytes 8388624 | tf_op jit(solution)/shard_map/all_gather | solution.py:137
  115.0 14.2 %copy.31 = bf16[1,1024,4,1024]{1,3,2,0:T(8,128)(2,1)} copy(bf16[1,1024,4,1024]{3,2,0,1:T(4,128)(2,1)} %all-gather.5.cloned.1.call-done) | data formatting | bytes 16777216 | tf_op jit(solution)/shard_map/reshape | solution.py:140
  129.1 21.9 %convolution_bitcast_fusion = f32[256,6,4,1024,1]{3,0,2,1,4:T(8,128)} fusion(bf16[1,1024,4,1024]{1,3,2,0:T(8,128)(2,1)} %copy.31, bf16[256,6,1024]{2,0,1:T(8,128)(2,1)} %collective-permute-done), kind=kOutput, calls=%fused_computation.7 | convolution fusion | flops 12884901888 | bytes 36700160 | tf_op jit(solution)/shard_map/dot_general | solution.py:138
  151.0 54.5 %fusion.2 = bf16[256,4,6,1024]{3,2,1,0:T(8,128)(2,1)} fusion(f32[256,6,4,1024,1]{3,0,2,1,4:T(8,128)} %convolution_bitcast_fusion, bf16[1,6,6,4,4]{2,4,3,1,0:T(4,128)(2,1)S(1)} %copy-done.5), kind=kOutput, calls=%fused_computation.3 | convolution fusion | flops 912261120 | bytes 37749888 | tf_op jit(solution)/shard_map/autc,uvst->asvc/dot_general | solution.py:143
  205.5 33.7 %all-gather.7.cloned.1.call-done = bf16[1,1024,6,1024]{3,1,2,0:T(8,128)(2,1)} async-done(((bf16[1,256,6,1024]{3,1,2,0:T(8,128)(2,1)}), bf16[1,1024,6,1024]{3,1,2,0:T(8,128)(2,1)}) %all-gather.7.cloned.1.call-update) | async-done | bytes 12582928 | tf_op jit(solution)/shard_map/all_gather | solution.py:149
  239.2 32.4 %fusion.9 = f32[256,4,1024]{2,0,1:T(8,128)S(1)} fusion(f32[256,4,1024]{2,0,1:T(8,128)} %fusion.19, bf16[1,1024,6,1024]{3,1,2,0:T(8,128)(2,1)} %all-gather.7.cloned.1.call-done, bf16[256,4,6,1024]{3,2,1,0:T(8,128)(2,1)} %fusion.2), kind=kOutput, calls=%fused_computation.10 | convolution fusion | flops 12886999040 | bytes 33554432 | tf_op jit(solution)/shard_map/asvc,cvy->asy/dot_general | solution.py:146
  271.7 4.7 %copy.24 = f32[256,4,1024]{2,1,0:T(4,128)} copy(f32[256,4,1024]{2,0,1:T(8,128)S(1)} %fusion.9) | data formatting | bytes 8388608 | tf_op jit(solution)/shard_map/sub | solution.py:161
  276.4 5.7 %reshape.19 = f32[1024,1024]{1,0:T(8,128)} reshape(f32[256,4,1024]{2,1,0:T(4,128)} %copy.24) | data formatting | bytes 8388608 | tf_op jit(solution)/shard_map/reshape | solution.py:161
  282.1 4.6 %fusion.33 = f32[256,1024]{1,0:T(8,128)S(1)} fusion(f32[1024,1024]{1,0:T(8,128)} %reshape.19), kind=kOutput, calls=%fused_computation.29 | convolution fusion | flops 1610612736 | bytes 6291456 | tf_op jit(solution)/shard_map/dot_general | solution.py:163
  286.7 1.8 fusion.10
  290.6 1.8 pad_maximum_fusion
  292.5 78.4 %all-reduce.2.cloned.1.call-done.packed_ref = f32[256,2560]{1,0:T(8,128)} async-done(((f32[256,2560]{1,0:T(8,128)}), f32[256,2560]{1,0:T(8,128)}) %all-reduce.2.cloned.1.call-update) | async-done | bytes 2621456 | tf_op jit(solution)/shard_map/psum | solution.py:171
  370.8 1.7 copy-done.2
  372.6 49.8 %factorize.1 = (f32[1024,1024]{1,0:T(8,128)S(1)}, f32[1024,1024]{1,0:T(8,128)S(1)}) custom-call(f32[256,2560]{1,0:T(8,128)S(1)} %copy-done.2), custom_call_target="tpu_custom_call" | custom-call | tf_op jit(solution)/shard_map/factorize/pallas_call | solution.py:117
  422.4 2.0 copy-done.3
  424.4 9.9 %multiply_convert_fusion = bf16[1024,1024]{1,0:T(8,128)(2,1)} fusion(f32[1024,1024]{1,0:T(8,128)} %reshape.19, f32[1024,1024]{1,0:T(8,128)S(1)} %get-tuple-element.4), kind=kOutput, calls=%fused_computation.11 | convolution fusion | flops 6444548096 | bytes 10485760 | tf_op jit(solution)/shard_map/dot_general | solution.py:174
  434.3 4.1 reshape.20
  438.4 2.3 multiply_bitcast_fusion
  (22 shorter events, 7.5 us)
Async XLA Ops:
  7.2 30.0 %copy-start = (bf16[1,1024,4,256]{3,2,1,0:T(4,128)(2,1)S(1)}, bf16[1,1024,4,256]{3,2,1,0:T(4,128)(2,1)}, u32[]{:S(2)}) copy-start(bf16[1,1024,4,256]{3,2,1,0:T(4,128)(2,1)} %param.10) | copy-start | bytes 6291460
  7.2 107.8 %all-gather.5.cloned.1.call-start = ((), (), s32[]{:S(2)}) async-start(), calls=%async_computation.2 | async-start | bytes 10485760 | tf_op jit(solution)/shard_map/all_gather | solution.py:137
  7.9 231.3 %all-gather.7.cloned.1.call-start = ((), (), s32[]{:S(2)}) async-start(), calls=%async_computation.3 | async-start | bytes 15728640 | tf_op jit(solution)/shard_map/all_gather | solution.py:149
  8.7 362.2 %all-reduce.2.cloned.1.call-start = ((), (), s32[]{:S(2)}) async-start(), calls=%async_computation.1 | async-start | bytes 5242880 | tf_op jit(solution)/shard_map/psum | solution.py:171
  8.7 28.5 %collective-permute-start.1 = (bf16[1024,1024]{1,0:T(8,128)(2,1)}, bf16[1024,1024]{1,0:T(8,128)(2,1)S(1)}, u32[]{:S(2)}, u32[]{:S(2)}) collective-permute-start(bf16[1024,1024]{1,0:T(8,128)(2,1)} %bitcast.71), channel_id=1, source_target_pairs={{28,0},{0,4},{4,8},{8,12},{12,16},{16,20},{20,24},{24,28},{29,1},{... | collective-permute-start | bytes 6291464 | tf_op jit(solution)/shard_map/ppermute | solution.py:20
  9.3 119.9 %collective-permute-start = (bf16[256,6,1024]{2,0,1:T(8,128)(2,1)}, bf16[256,6,1024]{2,0,1:T(8,128)(2,1)}, u32[]{:S(2)}, u32[]{:S(2)}) collective-permute-start(bf16[256,6,1024]{2,0,1:T(8,128)(2,1)} %bitcast.70), channel_id=1, source_target_pairs={{28,0},{0,4},{4,8},{8,12},{12,16},{16,20},{20,24},{24,28},{29,1},{... | collective-permute-start | bytes 9437192 | tf_op jit(solution)/shard_map/ppermute | solution.py:20
  129.1 21.9 %copy-start.5 = (bf16[1,6,6,4,4]{2,4,3,1,0:T(4,128)(2,1)S(1)}, bf16[1,6,6,4,4]{2,4,3,1,0:T(4,128)(2,1)}, u32[]{:S(2)}) copy-start(bf16[1,6,6,4,4]{2,4,3,1,0:T(4,128)(2,1)} %param.11) | copy-start | bytes 3460
  282.0 4.6 %copy-start.4 = (f32[1024,1024]{1,0:T(8,128)S(1)}, f32[1024,1024]{1,0:T(8,128)}, u32[]{:S(2)}) copy-start(f32[1024,1024]{1,0:T(8,128)} %reshape.19) | copy-start | bytes 12582916
  370.8 1.7 copy-start.2
  422.4 2.0 copy-start.3
  424.4 16.3 %copy-start.1 = (bf16[1,1024,4,256]{3,2,1,0:T(4,128)(2,1)S(1)}, bf16[1,1024,4,256]{3,2,1,0:T(4,128)(2,1)}, u32[]{:S(2)}) copy-start(bf16[1,1024,4,256]{3,2,1,0:T(4,128)(2,1)} %param.10) | copy-start | bytes 6291460
Sparse Core Ops, SparseCore 0:
  9.8 105.0 all-gather.4
  116.8 122.3 all-gather.6
  292.6 78.2 all-reduce.1

commit v2 on v1

--- a/solution.py
+++ b/solution.py
@@ -1,3 +1,4 @@
+import functools
 import math
 
 import jax
@@ -12,6 +13,9 @@
 BLOCK = 128
 STRIP = 256
 GROUP = 4
+TERMS = 2
+ROWS = 8
+WAVES = 2
 
 
 def shifted(block, axis, distance):
@@ -33,6 +37,78 @@
         return lax.dot_general(x, y, (dims, ((), ())), preferred_element_type=jnp.float32)
 
     return dot(a_high, b_high) + (dot(a_high, b_low) + dot(a_low, b_high))
+
+
+def reduce_kernel(n, own_ref, out_ref, parts, total, send_sem, recv_sem, send_back, recv_back):
+    me = lax.axis_index("bond")
+    barrier = pltpu.get_barrier_semaphore()
+    peers = [lax.rem(me + d, n) for d in range(1, n)]
+    for peer in peers:
+        pl.semaphore_signal(barrier, inc=1, device_id={"bond": peer})
+    pl.semaphore_wait(barrier, n - 1)
+    width = own_ref.shape[2] // WAVES
+    waves = [pl.ds(w * width, width) for w in range(WAVES)]
+    outward, back = [], []
+    for w, lanes in enumerate(waves):
+        outward.append([
+            pltpu.make_async_remote_copy(
+                src_ref=own_ref.at[peer, :, lanes],
+                dst_ref=parts.at[d, :, lanes],
+                send_sem=send_sem.at[w, d],
+                recv_sem=recv_sem.at[w, d],
+                device_id={"bond": peer},
+            )
+            for d, peer in enumerate(peers)
+        ])
+        for copy in outward[w]:
+            copy.start()
+    for w, lanes in enumerate(waves):
+        for copy in outward[w]:
+            copy.wait_recv()
+        value = own_ref[me, :, lanes]
+        for d in range(n - 1):
+            value = value + parts[d, :, lanes]
+        total[me, :, lanes] = value
+        back.append([
+            pltpu.make_async_remote_copy(
+                src_ref=total.at[me, :, lanes],
+                dst_ref=total.at[me, :, lanes],
+                send_sem=send_back.at[w, d],
+                recv_sem=recv_back.at[w, d],
+                device_id={"bond": peer},
+            )
+            for d, peer in enumerate(peers)
+        ])
+        for copy in back[w]:
+            copy.start()
+    for w, lanes in enumerate(waves):
+        for copy in back[w]:
+            copy.wait_recv()
+        out_ref[:, :, lanes] = total[:, :, lanes]
+    for copies in outward + back:
+        for copy in copies:
+            copy.wait_send()
+
+
+def summed(packed):
+    n = lax.axis_size("bond")
+    rows, width = packed.shape
+    shape = (n, rows // n, width)
+    return pl.pallas_call(
+        functools.partial(reduce_kernel, n),
+        out_shape=jax.ShapeDtypeStruct(shape, jnp.float32),
+        in_specs=[pl.BlockSpec(memory_space=pltpu.VMEM)],
+        out_specs=pl.BlockSpec(memory_space=pltpu.VMEM),
+        scratch_shapes=[
+            pltpu.VMEM((n - 1,) + shape[1:], jnp.float32),
+            pltpu.VMEM(shape, jnp.float32),
+        ]
+        + [pltpu.SemaphoreType.DMA((WAVES, n - 1))] * 4,
+        compiler_params=pltpu.CompilerParams(
+            collective_id=0, has_side_effects=True, vmem_limit_bytes=24 * 2**20
+        ),
+        name="summed",
+    )(packed.reshape(shape)).reshape(rows, width)
 
 
 def eliminate(block, rows_ref):
@@ -129,36 +205,89 @@
     )(packed)
 
 
+def mix_kernel(spread_ref, projected_ref, mixture_ref):
+    width = projected_ref.shape[2] // PHYS
+    spread = spread_ref[...]
+    results = []
+    for first in range(0, 2 * ROWS, ROWS):
+        stack = jnp.concatenate(
+            [
+                projected_ref[u, first : first + ROWS, t * width : (t + 1) * width]
+                for u in range(MPOB)
+                for t in range(PHYS)
+            ],
+            axis=0,
+        )
+        high, low = halves(stack)
+        results.append(
+            jnp.dot(spread, high, preferred_element_type=jnp.float32)
+            + jnp.dot(spread, low, preferred_element_type=jnp.float32)
+        )
+    for v in range(MPOB):
+        for s in range(PHYS):
+            at = (v * PHYS + s) * ROWS
+            both = jnp.concatenate([part[at : at + ROWS, :] for part in results], axis=0)
+            mixture_ref[v, s] = both.astype(jnp.bfloat16)
+
+
+def mixed(projected, coupling):
+    own_rows, width = projected.shape[1], projected.shape[2] // PHYS
+    side = MPOB * PHYS * ROWS
+    diagonal = jnp.eye(ROWS, dtype=coupling.dtype)
+    turned = jnp.transpose(coupling, (1, 2, 0, 3))
+    spread = turned[:, :, None, :, :, None] * diagonal[None, None, :, None, None, :]
+    return pl.pallas_call(
+        mix_kernel,
+        grid=(own_rows // (2 * ROWS),),
+        out_shape=jax.ShapeDtypeStruct((MPOB, PHYS, own_rows, width), jnp.bfloat16),
+        in_specs=[
+            pl.BlockSpec((side, side), lambda i: (0, 0)),
+            pl.BlockSpec((MPOB, 2 * ROWS, PHYS * width), lambda i: (0, i, 0)),
+        ],
+        out_specs=pl.BlockSpec((MPOB, PHYS, 2 * ROWS, width), lambda i: (0, 0, i, 0)),
+        compiler_params=pltpu.CompilerParams(vmem_limit_bytes=40 * 2**20),
+        cost_estimate=pl.CostEstimate(
+            flops=4 * side * MPOB * PHYS * own_rows * width,
+            bytes_accessed=6 * MPOB * PHYS * own_rows * width,
+            transcendentals=0,
+        ),
+        name="mixed",
+    )(spread.reshape(side, side), projected)
+
+
 def shards(left_env, prev_left, cur_site, prev_site, hamiltonian, right_env, prev_right):
     left_now, prev_now = shifted((left_env[0], prev_left[0]), "seg", 1)
     own_rows = left_now.shape[0]
     bond_width = left_now.shape[2]
-    coupling = hamiltonian[0].astype(jnp.float32)
     current = lax.all_gather(cur_site[0], "bond", axis=0, tiled=True)
+    left_terms = jnp.transpose(left_now, (1, 0, 2)).reshape(MPOB * own_rows, bond_width)
     projected = jnp.dot(
-        left_now.reshape(own_rows * MPOB, bond_width),
+        left_terms,
         current.reshape(bond_width, PHYS * bond_width),
         preferred_element_type=jnp.float32,
-    ).reshape(own_rows, MPOB, PHYS, bond_width)
-    mixture = jnp.einsum(
-        "autc,uvst->asvc", projected, coupling, precision=lax.Precision.HIGH
-    ).astype(jnp.bfloat16)
-    applied = jnp.einsum(
-        "asvc,cvy->asy",
-        mixture,
-        lax.all_gather(right_env[0], "bond", axis=0, tiled=True),
-        preferred_element_type=jnp.float32,
-    )
+    ).reshape(MPOB, own_rows, PHYS * bond_width)
+    mixture = mixed(projected, hamiltonian[0])
     partial_value = jnp.einsum(
         "ab,bsc->asc", prev_now, prev_site[0], preferred_element_type=jnp.float32
     ).astype(jnp.bfloat16)
     second = jnp.einsum(
-        "akc,cy->aky",
+        "akc,cy->kay",
         lax.all_to_all(partial_value, "bond", split_axis=0, concat_axis=2, tiled=True),
         prev_right[0],
         preferred_element_type=jnp.float32,
     )
-    target = (2.0 * applied - second).reshape(own_rows * PHYS, bond_width)
+    flat_rows = own_rows * PHYS
+    right_terms = jnp.transpose(right_env[0], (1, 0, 2))
+    applied = 0.0
+    for start in range(0, MPOB, TERMS):
+        right = lax.all_gather(right_terms[start : start + TERMS], "bond", axis=1, tiled=True)
+        for v in range(TERMS):
+            applied += jnp.dot(
+                mixture[start + v].reshape(flat_rows, bond_width),
+                right[v],
+                preferred_element_type=jnp.float32,
+            )
+    target = 2.0 * applied - second.reshape(flat_rows, bond_width)
     strips = [
         jnp.dot(
             target[:, start : start + STRIP].T,
@@ -168,7 +297,7 @@
         )
         for start in range(0, bond_width, STRIP)
     ]
-    packed = lax.psum(jnp.concatenate(strips, axis=1), "bond")
+    packed = summed(jnp.concatenate(strips, axis=1))
     upper, inverse = factorize(packed, bond_width)
     norming = math.sqrt(bond_width * PHYS)
     solved = lax.dot_general(
@@ -178,7 +307,8 @@
         precision=lax.Precision.HIGH,
         preferred_element_type=jnp.float32,
     )
-    new_site = (solved * norming).astype(jnp.bfloat16).reshape(1, own_rows, PHYS, bond_width)
+    new_site = (solved * norming).astype(jnp.bfloat16).reshape(PHYS, own_rows, bond_width)
+    new_site = jnp.transpose(new_site, (1, 0, 2))[None]
     offset = lax.axis_index("bond") * own_rows
     center = lax.dynamic_slice_in_dim(upper, offset, own_rows, 0) / norming
     return (new_site, center[None])

time: 451 us -> 439 us (0.973)
  Pallas kernels: 49.8 us -> 128 us
  matrix products: 136 us -> 81.1 us
  blocking collectives: 41.1 us -> 0 us
  starting transfers between devices: 3.33 us -> 7.96 us
    psum x1 -> x0, waiting for transfers between devices: 78.4 us -> none  [shards(): packed = lax.psum(jnp.concatenate(strips, axis=1), 'bond')]
    pallas_call x0 -> x2, Pallas kernels: none -> 77.7 us  [the longest x1 59.9 us: summed(): pl.pallas_call(functools.partial(reduce_kernel, n), out_shape=jax.ShapeDt...]
    dot_general x4 -> x8, matrix products: 115 us -> 65.1 us  [the longest x6 37.5 us: shards(): jnp.dot(mixture[start + v].reshape(flat_rows, bond_width), right[v], pref...]
    all_gather x1 -> x3, waiting for transfers between devices: 33.7 us -> 83.1 us  [shards(): lax.all_gather(right_terms[start:start + TERMS], 'bond', axis=1, tiled=True)]
    all_to_all x0 -> x1, waiting for transfers between devices: none -> 43 us  [shards(): lax.all_to_all(partial_value, 'bond', split_axis=0, concat_axis=2, tiled=...]
    all_to_all x1 -> x0, blocking collectives: 41.1 us -> none  [shards(): lax.all_to_all(partial_value, 'bond', split_axis=0, concat_axis=2, tiled=...]
    all_gather x1, waiting for transfers between devices: 21.9 us -> 7.4 us  [shards(): current = lax.all_gather(cur_site[0], 'bond', axis=0, tiled=True)]
    slice x0 -> x2, local copies, waits for them, and re-layouts: none -> 7.84 us  [the longest x1 4.21 us: shards(): mixture[start + v].reshape(flat_rows, bond_width)]
  transfers between devices with their start and end apart: 5 -> 7, of which waited for: 4 -> 5; matrix products, arithmetic and copies ran while one was open for 23% -> 19% of each run, Pallas kernels for 0% -> 4%
where the time goes in v2:
time: 439 us; the launch traced here: 432 us
  waiting for transfers between devices  161 us (37%)
  Pallas kernels  128 us (29%)
  matrix products  81.1 us (18%)
  local copies, waits for them, and re-layouts  38.7 us (9%)
  between operations  14.5 us (3%)
  starting transfers between devices  7.96 us (2%)
    all_gather x3, waiting for transfers between devices, shards(): lax.all_gather(right_terms[start:start + TERMS], 'bond', axis=1, tiled=True)  83.1 us
    pallas_call x1, Pallas kernels, summed(): pl.pallas_call(functools.partial(reduce_kernel, n), out_shape=jax.ShapeDt...  59.9 us
    pallas_call x1, Pallas kernels, factorize(): pl.pallas_call(factor_kernel, out_shape=(whole, whole), in_specs=[pl.Bloc...  49.8 us
    all_to_all x1, waiting for transfers between devices, shards(): lax.all_to_all(partial_value, 'bond', split_axis=0, concat_axis=2, tiled=...  43 us
    dot_general x6, matrix products, shards(): jnp.dot(mixture[start + v].reshape(flat_rows, bond_width), right[v], pref...  37.5 us
    ppermute x2, waiting for transfers between devices, shifted(): return lax.ppermute(block, axis, route)  25.3 us
    dot_general x1, matrix products, shards(): jnp.dot(left_terms, current.reshape(bond_width, PHYS * bond_width), prefe...  21.1 us
    pallas_call x1, Pallas kernels, mixed(): pl.pallas_call(mix_kernel, grid=(own_rows // (2 * ROWS),), out_shape=jax....  17.8 us
  transfers between devices with their start and end apart: 7, of which 5 were waited for; matrix products, arithmetic and copies ran while one was open for 19% of the time, Pallas kernels for 4%

profile of v2, /device:TPU:0, one launch (start us, length us, event | category | flops | bytes accessed | tf_op | source)
XLA Modules:
  0.0 432.5 jit_solution(7594115501413741333)
XLA Ops:
  8.0 3.6 fusion.30
  15.6 25.3 %collective-permute-done.1 = bf16[1024,1024]{1,0:T(8,128)(2,1)S(1)} collective-permute-done((bf16[1024,1024]{1,0:T(8,128)(2,1)}, bf16[1024,1024]{1,0:T(8,128)(2,1)S(1)}, u32[]{:S(2)}, u32[]{:S(2)}) %collective-permute-start.1) | collective-permute-done | bytes 2097184 | tf_op jit(solution)/shard_map/ppermute | solution.py:24
  43.2 2.9 copy.17
  46.1 4.6 %all-to-all-start = ((bf16[1024,4,256]{2,1,0:T(4,128)(2,1)}), bf16[1024,4,256]{2,1,0:T(4,128)(2,1)}, u32[]{:S(2)}, u32[]{:S(2)}) async-start(bf16[1024,4,256]{2,1,0:T(4,128)(2,1)} %copy.17), calls=%async_computation | async-start | bytes 4194304 | tf_op jit(solution)/shard_map/all_to_all | solution.py:275
  53.1 43.0 %all-to-all-done = bf16[1024,4,256]{2,1,0:T(4,128)(2,1)} async-done(((bf16[1024,4,256]{2,1,0:T(4,128)(2,1)}), bf16[1024,4,256]{2,1,0:T(4,128)(2,1)}, u32[]{:S(2)}, u32[]{:S(2)}) %all-to-all-start) | async-done | bytes 2097184 | tf_op jit(solution)/shard_map/all_to_all | solution.py:275
  96.1 4.5 %copy.29 = bf16[4,256,4,256]{3,0,1,2:T(4,128)(2,1)} copy(bf16[4,256,4,256]{3,2,1,0:T(4,128)(2,1)} %bitcast.23) | data formatting | bytes 4194304 | tf_op jit(solution)/shard_map/all_to_all | solution.py:275
  100.7 4.7 %all_to_all.16 = bf16[256,4,1024]{2,0,1:T(8,128)(2,1)} reshape(bf16[256,4,4,256]{3,2,0,1:T(4,128)(2,1)} %bitcast.85) | data formatting | bytes 4194304 | tf_op jit(solution)/shard_map/all_to_all | solution.py:275
  105.3 6.5 %fusion.12 = f32[256,4,1024]{2,0,1:T(8,128)} fusion(bf16[256,4,1024]{2,0,1:T(8,128)(2,1)} %all_to_all.16, bf16[1,1024,1024]{2,1,0:T(8,128)(2,1)} %param.13), kind=kOutput, calls=%fused_computation.21 | convolution fusion | flops 2147483648 | bytes 8388608 | tf_op jit(solution)/shard_map/akc,cy->kay/dot_general | solution.py:273
  111.8 7.4 %all-gather.12.cloned.1.call-done = bf16[1,1024,4,1024]{3,2,0,1:T(4,128)(2,1)} async-done(((bf16[1,256,4,1024]{3,2,0,1:T(4,128)(2,1)}), bf16[1,1024,4,1024]{3,2,0,1:T(4,128)(2,1)}) %all-gather.12.cloned.1.call-update) | async-done | bytes 8388624 | tf_op jit(solution)/shard_map/all_gather | solution.py:262
  119.2 14.6 %reshape.43 = bf16[1024,4096,1]{1,0,2:T(8,128)(2,1)} reshape(bf16[1,1024,4,1024]{3,2,0,1:T(4,128)(2,1)} %all-gather.12.cloned.1.call-done) | data formatting | bytes 16777216 | tf_op jit(solution)/shard_map/reshape | solution.py:266
  133.8 21.1 %fusion.2.projected_ref = f32[6,256,4096]{2,1,0:T(8,128)} fusion(bf16[1024,4096,1]{1,0,2:T(8,128)(2,1)} %reshape.43, bf16[256,6,1024]{2,0,1:T(8,128)(2,1)} %collective-permute-done), kind=kOutput, calls=%fused_computation.4 | convolution fusion | flops 12884901888 | bytes 36700160 | tf_op jit(solution)/shard_map/dot_general | solution.py:264
  155.0 17.8 %mixed.1 = bf16[6,4,256,1024]{3,2,1,0:T(8,128)(2,1)S(1)} custom-call(bf16[192,192]{1,0:T(8,128)(2,1)S(1)} %mul.35.spread_ref, f32[6,256,4096]{2,1,0:T(8,128)} %fusion.2.projected_ref), custom_call_target="tpu_custom_call" | custom-call | flops 4831838208 | bytes 37748736 | tf_op jit(solution)/shard_map/mixed/pallas_call | solution.py:239
  172.8 4.2 fusion.29
  177.1 6.7 %fusion.6 = f32[1024,1024]{1,0:T(8,128)} fusion(bf16[1024,1024]{1,0:T(8,128)(2,1)} %bitcast.91, bf16[2,1024,1024]{2,1,0:T(8,128)(2,1)} %all-gather.10.cloned.1.call-done), kind=kOutput, calls=%fused_computation.10 | convolution fusion | flops 2147483648 | bytes 8388608 | tf_op jit(solution)/shard_map/dot_general | solution.py:285
  183.7 4.4 %fusion.7 = f32[1024,1024]{1,0:T(8,128)} fusion(bf16[1024,1024]{1,0:T(8,128)(2,1)S(1)} %bitcast.90, bf16[2,1024,1024]{2,1,0:T(8,128)(2,1)S(1)} %copy-done.8), kind=kOutput, calls=%fused_computation.12 | convolution fusion | flops 2147483648 | bytes 8388608 | tf_op jit(solution)/shard_map/dot_general | solution.py:285
  188.1 39.3 %all-gather.8.cloned.1.call-done = bf16[2,1024,1024]{2,1,0:T(8,128)(2,1)} async-done(((bf16[2,256,1024]{2,1,0:T(8,128)(2,1)}), bf16[2,1024,1024]{2,1,0:T(8,128)(2,1)}) %all-gather.8.cloned.1.call-update) | async-done | bytes 4194320 | tf_op jit(solution)/shard_map/all_gather | solution.py:283
  227.4 6.7 %fusion.8 = f32[1024,1024]{1,0:T(8,128)} fusion(bf16[1024,1024]{1,0:T(8,128)(2,1)} %bitcast.89, bf16[2,1024,1024]{2,1,0:T(8,128)(2,1)} %all-gather.8.cloned.1.call-done), kind=kOutput, calls=%fused_computation.14 | convolution fusion | flops 2147483648 | bytes 8388608 | tf_op jit(solution)/shard_map/dot_general | solution.py:285
  234.1 4.3 %fusion.9 = f32[1024,1024]{1,0:T(8,128)} fusion(bf16[1024,1024]{1,0:T(8,128)(2,1)S(1)} %bitcast.88, bf16[2,1024,1024]{2,1,0:T(8,128)(2,1)S(1)} %copy-done.9), kind=kOutput, calls=%fused_computation.16 | convolution fusion | flops 2147483648 | bytes 8388608 | tf_op jit(solution)/shard_map/dot_general | solution.py:285
  238.4 43.8 %all-gather.6.cloned.1.call-done = bf16[2,1024,1024]{2,1,0:T(8,128)(2,1)} async-done(((bf16[2,256,1024]{2,1,0:T(8,128)(2,1)}), bf16[2,1024,1024]{2,1,0:T(8,128)(2,1)}) %all-gather.6.cloned.1.call-update) | async-done | bytes 4194320 | tf_op jit(solution)/shard_map/all_gather | solution.py:283
  282.3 6.6 %fusion.10 = f32[1024,1024]{1,0:T(8,128)} fusion(bf16[1024,1024]{1,0:T(8,128)(2,1)} %bitcast.87, bf16[2,1024,1024]{2,1,0:T(8,128)(2,1)} %all-gather.6.cloned.1.call-done), kind=kOutput, calls=%fused_computation.18 | convolution fusion | flops 2147483648 | bytes 8388608 | tf_op jit(solution)/shard_map/dot_general | solution.py:285
  288.9 8.8 %bitcast_subtract_fusion = f32[1024,1024]{1,0:T(8,128)S(1)} fusion(f32[256,4,1024]{2,0,1:T(8,128)S(1)} %copy-done.2, f32[1024,1024]{1,0:T(8,128)S(1)} %copy-done.3, f32[1024,1024]{1,0:T(8,128)S(1)} %copy-done.4, f32[1024,1024]{1,0:T(8,128)} %fusion.8, f32[1024,1024]{1,0:T(8,128)} %fusion.9, f32[1024,1024]{1,0:T(8,128)} %fusion.10, ...), kind=kOutput, calls=%fused_computation | convolution fusion | flops 2154823680 | bytes 33554432 | tf_op jit(solution)/shard_map/dot_general | solution.py:285
  304.4 59.9 %summed.1 = f32[4,64,2560]{2,1,0:T(8,128)S(1)} custom-call(f32[4,64,2560]{2,1,0:T(8,128)S(1)} %bitcast.82), custom_call_target="tpu_custom_call" | custom-call | tf_op jit(solution)/shard_map/summed/pallas_call | solution.py:97
  364.3 49.8 %factorize.1 = (f32[1024,1024]{1,0:T(8,128)S(1)}, f32[1024,1024]{1,0:T(8,128)S(1)}) custom-call(f32[256,2560]{1,0:T(8,128)S(1)} %bitcast.83), custom_call_target="tpu_custom_call" | custom-call | tf_op jit(solution)/shard_map/factorize/pallas_call | solution.py:193
  414.1 7.3 %multiply_convert_fusion = bf16[1024,1024]{1,0:T(8,128)(2,1)S(1)} fusion(f32[1024,1024]{1,0:T(8,128)S(1)} %bitcast_subtract_fusion, f32[1024,1024]{1,0:T(8,128)S(1)} %get-tuple-element.4), kind=kOutput, calls=%fused_computation.1 | convolution fusion | flops 6444548096 | bytes 10485760 | tf_op jit(solution)/shard_map/dot_general | solution.py:303
  (44 shorter events, 20.0 us)
Async XLA Ops:
  7.2 33.7 %copy-start = (bf16[1,1024,4,256]{3,2,1,0:T(4,128)(2,1)S(1)}, bf16[1,1024,4,256]{3,2,1,0:T(4,128)(2,1)}, u32[]{:S(2)}) copy-start(bf16[1,1024,4,256]{3,2,1,0:T(4,128)(2,1)} %param.10) | copy-start | bytes 6291460
  7.2 112.0 %all-gather.12.cloned.1.call-start = ((), (), s32[]{:S(2)}) async-start(), calls=%async_computation.4 | async-start | bytes 10485760 | tf_op jit(solution)/shard_map/all_gather | solution.py:262
  7.9 169.1 %all-gather.10.cloned.1.call-start = ((), (), s32[]{:S(2)}) async-start(), calls=%async_computation.3 | async-start | bytes 5242880 | tf_op jit(solution)/shard_map/all_gather | solution.py:283
  11.6 215.8 %all-gather.8.cloned.1.call-start = ((), (), s32[]{:S(2)}) async-start(), calls=%async_computation.2 | async-start | bytes 5242880 | tf_op jit(solution)/shard_map/all_gather | solution.py:283
  12.4 28.5 %collective-permute-start.1 = (bf16[1024,1024]{1,0:T(8,128)(2,1)}, bf16[1024,1024]{1,0:T(8,128)(2,1)S(1)}, u32[]{:S(2)}, u32[]{:S(2)}) collective-permute-start(bf16[1024,1024]{1,0:T(8,128)(2,1)} %bitcast.97), channel_id=1, source_target_pairs={{28,0},{0,4},{4,8},{8,12},{12,16},{16,20},{20,24},{24,28},{29,1},{... | collective-permute-start | bytes 6291464 | tf_op jit(solution)/shard_map/ppermute | solution.py:24
  12.9 120.9 %collective-permute-start = (bf16[256,6,1024]{2,0,1:T(8,128)(2,1)}, bf16[256,6,1024]{2,0,1:T(8,128)(2,1)}, u32[]{:S(2)}, u32[]{:S(2)}) collective-permute-start(bf16[256,6,1024]{2,0,1:T(8,128)(2,1)} %bitcast.96), channel_id=1, source_target_pairs={{28,0},{0,4},{4,8},{8,12},{12,16},{16,20},{20,24},{24,28},{29,1},{... | collective-permute-start | bytes 9437192 | tf_op jit(solution)/shard_map/ppermute | solution.py:24
  46.1 5.2 %copy-start.7 = (bf16[1,6,6,4,4]{2,4,3,1,0:T(4,128)(2,1)S(1)}, bf16[1,6,6,4,4]{2,4,3,1,0:T(4,128)(2,1)}, u32[]{:S(2)}) copy-start(bf16[1,6,6,4,4]{2,4,3,1,0:T(4,128)(2,1)} %param.11) | copy-start | bytes 3460
  46.1 50.0 %all-to-all-start = ((bf16[1024,4,256]{2,1,0:T(4,128)(2,1)}), bf16[1024,4,256]{2,1,0:T(4,128)(2,1)}, u32[]{:S(2)}, u32[]{:S(2)}) async-start(bf16[1024,4,256]{2,1,0:T(4,128)(2,1)} %copy.17), calls=%async_computation | async-start | bytes 4194304 | tf_op jit(solution)/shard_map/all_to_all | solution.py:275
  50.7 231.6 %all-gather.6.cloned.1.call-start = ((), (), s32[]{:S(2)}) async-start(), calls=%async_computation.1 | async-start | bytes 5242880 | tf_op jit(solution)/shard_map/all_gather | solution.py:283
  177.1 6.7 %copy-start.6 = (bf16[1,4,256,1024]{3,2,1,0:T(8,128)(2,1)S(1)}, bf16[1,4,256,1024]{3,2,1,0:T(8,128)(2,1)}, u32[]{:S(2)}) copy-start(bf16[1,4,256,1024]{3,2,1,0:T(8,128)(2,1)} %get-tuple-element.8) | copy-start | bytes 6291460
  177.1 6.7 %copy-start.8 = (bf16[2,1024,1024]{2,1,0:T(8,128)(2,1)S(1)}, bf16[2,1024,1024]{2,1,0:T(8,128)(2,1)}, u32[]{:S(2)}) copy-start(bf16[2,1024,1024]{2,1,0:T(8,128)(2,1)} %all-gather.10.cloned.1.call-done) | copy-start | bytes 12582916
  227.4 6.7 %copy-start.5 = (bf16[1,4,256,1024]{3,2,1,0:T(8,128)(2,1)S(1)}, bf16[1,4,256,1024]{3,2,1,0:T(8,128)(2,1)}, u32[]{:S(2)}) copy-start(bf16[1,4,256,1024]{3,2,1,0:T(8,128)(2,1)} %get-tuple-element.10) | copy-start | bytes 6291460
  227.4 6.7 %copy-start.9 = (bf16[2,1024,1024]{2,1,0:T(8,128)(2,1)S(1)}, bf16[2,1024,1024]{2,1,0:T(8,128)(2,1)}, u32[]{:S(2)}) copy-start(bf16[2,1024,1024]{2,1,0:T(8,128)(2,1)} %all-gather.8.cloned.1.call-done) | copy-start | bytes 12582916
  282.3 6.7 %copy-start.2 = (f32[256,4,1024]{2,0,1:T(8,128)S(1)}, f32[256,4,1024]{2,0,1:T(8,128)}, u32[]{:S(2)}) copy-start(f32[256,4,1024]{2,0,1:T(8,128)} %fusion.12) | copy-start | bytes 12582916
  282.3 6.7 %copy-start.3 = (f32[1024,1024]{1,0:T(8,128)S(1)}, f32[1024,1024]{1,0:T(8,128)}, u32[]{:S(2)}) copy-start(f32[1024,1024]{1,0:T(8,128)} %fusion.6) | copy-start | bytes 12582916
  282.3 6.7 %copy-start.4 = (f32[1024,1024]{1,0:T(8,128)S(1)}, f32[1024,1024]{1,0:T(8,128)}, u32[]{:S(2)}) copy-start(f32[1024,1024]{1,0:T(8,128)} %fusion.7) | copy-start | bytes 12582916
  421.5 4.0 copy-start.1
Sparse Core Ops, SparseCore 0:
  9.8 109.3 all-gather.11
  121.1 51.8 all-gather.9
  174.8 52.5 all-gather.7
  229.7 52.5 all-gather.5

commit v3 on v2

--- a/solution.py
+++ b/solution.py
@@ -13,7 +13,6 @@
 BLOCK = 128
 STRIP = 256
 GROUP = 4
-TERMS = 2
 ROWS = 8
 WAVES = 2
 
@@ -205,7 +204,7 @@
     )(packed)
 
 
-def mix_kernel(spread_ref, projected_ref, mixture_ref):
+def mix_kernel(parts, spread_ref, projected_ref, mixture_ref):
     width = projected_ref.shape[2] // PHYS
     spread = spread_ref[...]
     results = []
@@ -226,25 +225,29 @@
     for v in range(MPOB):
         for s in range(PHYS):
             at = (v * PHYS + s) * ROWS
-            both = jnp.concatenate([part[at : at + ROWS, :] for part in results], axis=0)
-            mixture_ref[v, s] = both.astype(jnp.bfloat16)
-
-
-def mixed(projected, coupling):
+            both = jnp.concatenate([one[at : at + ROWS, :] for one in results], axis=0)
+            both = both.astype(jnp.bfloat16)
+            part = width // parts
+            for p in range(parts):
+                start = (p * MPOB + v) * part
+                mixture_ref[s, :, start : start + part] = both[:, p * part : (p + 1) * part]
+
+
+def mixed(projected, coupling, parts):
     own_rows, width = projected.shape[1], projected.shape[2] // PHYS
     side = MPOB * PHYS * ROWS
     diagonal = jnp.eye(ROWS, dtype=coupling.dtype)
     turned = jnp.transpose(coupling, (1, 2, 0, 3))
     spread = turned[:, :, None, :, :, None] * diagonal[None, None, :, None, None, :]
     return pl.pallas_call(
-        mix_kernel,
+        functools.partial(mix_kernel, parts),
         grid=(own_rows // (2 * ROWS),),
-        out_shape=jax.ShapeDtypeStruct((MPOB, PHYS, own_rows, width), jnp.bfloat16),
+        out_shape=jax.ShapeDtypeStruct((PHYS, own_rows, MPOB * width), jnp.bfloat16),
         in_specs=[
             pl.BlockSpec((side, side), lambda i: (0, 0)),
             pl.BlockSpec((MPOB, 2 * ROWS, PHYS * width), lambda i: (0, i, 0)),
         ],
-        out_specs=pl.BlockSpec((MPOB, PHYS, 2 * ROWS, width), lambda i: (0, 0, i, 0)),
+        out_specs=pl.BlockSpec((PHYS, 2 * ROWS, MPOB * width), lambda i: (0, i, 0)),
         compiler_params=pltpu.CompilerParams(vmem_limit_bytes=40 * 2**20),
         cost_estimate=pl.CostEstimate(
             flops=4 * side * MPOB * PHYS * own_rows * width,
@@ -266,7 +269,8 @@
         current.reshape(bond_width, PHYS * bond_width),
         preferred_element_type=jnp.float32,
     ).reshape(MPOB, own_rows, PHYS * bond_width)
-    mixture = mixed(projected, hamiltonian[0])
+    parts = lax.axis_size("bond") if own_rows % 128 == 0 else 1
+    mixture = mixed(projected, hamiltonian[0], parts)
     partial_value = jnp.einsum(
         "ab,bsc->asc", prev_now, prev_site[0], preferred_element_type=jnp.float32
     ).astype(jnp.bfloat16)
@@ -278,15 +282,17 @@
     )
     flat_rows = own_rows * PHYS
     right_terms = jnp.transpose(right_env[0], (1, 0, 2))
-    applied = 0.0
-    for start in range(0, MPOB, TERMS):
-        right = lax.all_gather(right_terms[start : start + TERMS], "bond", axis=1, tiled=True)
-        for v in range(TERMS):
-            applied += jnp.dot(
-                mixture[start + v].reshape(flat_rows, bond_width),
-                right[v],
-                preferred_element_type=jnp.float32,
-            )
+    if parts > 1:
+        right = lax.all_gather(
+            right_terms.reshape(MPOB * own_rows, bond_width), "bond", axis=0, tiled=True
+        )
+    else:
+        right = lax.all_gather(right_terms, "bond", axis=1, tiled=True)
+    applied = jnp.dot(
+        mixture.reshape(flat_rows, MPOB * bond_width),
+        right.reshape(MPOB * bond_width, bond_width),
+        preferred_element_type=jnp.float32,
+    )
     target = 2.0 * applied - second.reshape(flat_rows, bond_width)
     strips = [
         jnp.dot(

time: 439 us -> 393 us (0.90); the launches traced: 432 us -> 392 us
  matrix products: 81.1 us -> 61.7 us
  waiting for transfers between devices: 161 us -> 142 us
    all_gather x3 -> x1, waiting for transfers between devices: 83.1 us -> 63.9 us  [shards(): lax.all_gather(right_terms.reshape(MPOB * own_rows, bond_width), 'bond',...]
    dot_general x6 -> x1, matrix products: 37.5 us -> 19.1 us  [shards(): jnp.dot(mixture.reshape(flat_rows, MPOB * bond_width), right.reshape(MPOB...]
    all_gather x1, waiting for transfers between devices: 7.4 us -> 19.5 us  [shards(): current = lax.all_gather(cur_site[0], 'bond', axis=0, tiled=True)]
    all_to_all x1, waiting for transfers between devices: 43 us -> 31.6 us  [shards(): lax.all_to_all(partial_value, 'bond', split_axis=0, concat_axis=2, tiled=...]
    slice x2 -> x0, local copies, waits for them, and re-layouts: 7.84 us -> none  [the longest x1 4.21 us: shards(): mixture[start + v].reshape(flat_rows, bond_width)]
    unnamed x20 -> x8, local copies, waits for them, and re-layouts: 0.05 us -> 5.97 us
  transfers between devices with their start and end apart: 7 -> 5, of which waited for: 5 -> 4; matrix products, arithmetic and copies ran while one was open for 19% -> 14% of each run, Pallas kernels for 4% -> 5%
where the time goes in v3:
time: 393 us; the launch traced here: 392 us
  waiting for transfers between devices  142 us (36%)
  Pallas kernels  128 us (33%)
  matrix products  61.7 us (16%)
  local copies, waits for them, and re-layouts  36.6 us (9%)
  between operations  14.2 us (4%)
  starting transfers between devices  8.05 us (2%)
    all_gather x1, waiting for transfers between devices, shards(): lax.all_gather(right_terms.reshape(MPOB * own_rows, bond_width), 'bond',...  63.9 us
    pallas_call x1, Pallas kernels, summed(): pl.pallas_call(functools.partial(reduce_kernel, n), out_shape=jax.ShapeDt...  59.8 us
    pallas_call x1, Pallas kernels, factorize(): pl.pallas_call(factor_kernel, out_shape=(whole, whole), in_specs=[pl.Bloc...  50.2 us
    all_to_all x1, waiting for transfers between devices, shards(): lax.all_to_all(partial_value, 'bond', split_axis=0, concat_axis=2, tiled=...  31.6 us
    ppermute x2, waiting for transfers between devices, shifted(): return lax.ppermute(block, axis, route)  25.3 us
    dot_general x1, matrix products, shards(): jnp.dot(left_terms, current.reshape(bond_width, PHYS * bond_width), prefe...  21.2 us
    all_gather x1, waiting for transfers between devices, shards(): current = lax.all_gather(cur_site[0], 'bond', axis=0, tiled=True)  19.5 us
    dot_general x1, matrix products, shards(): jnp.dot(mixture.reshape(flat_rows, MPOB * bond_width), right.reshape(MPOB...  19.1 us
  transfers between devices with their start and end apart: 5, of which 4 were waited for; matrix products, arithmetic and copies ran while one was open for 14% of the time, Pallas kernels for 5%

profile of v3, /device:TPU:0, one launch (start us, length us, event | category | flops | bytes accessed | tf_op | source)
XLA Modules:
  0.0 392.1 jit_solution(15401734456700709113)
XLA Ops:
  9.2 2.7 collective-permute-start
  11.9 25.3 %collective-permute-done.1 = bf16[1024,1024]{1,0:T(8,128)(2,1)S(1)} collective-permute-done((bf16[1024,1024]{1,0:T(8,128)(2,1)}, bf16[1024,1024]{1,0:T(8,128)(2,1)S(1)}, u32[]{:S(2)}, u32[]{:S(2)}) %collective-permute-start.1) | collective-permute-done | bytes 2097184 | tf_op jit(solution)/shard_map/ppermute | solution.py:23
  37.2 2.3 fusion.11
  39.5 2.9 copy.17
  42.4 4.8 %all-to-all-start = ((bf16[1024,4,256]{2,1,0:T(4,128)(2,1)}), bf16[1024,4,256]{2,1,0:T(4,128)(2,1)}, u32[]{:S(2)}, u32[]{:S(2)}) async-start(bf16[1024,4,256]{2,1,0:T(4,128)(2,1)} %copy.17), calls=%async_computation | async-start | bytes 4194304 | tf_op jit(solution)/shard_map/all_to_all | solution.py:279
  49.0 31.6 %all-to-all-done = bf16[1024,4,256]{2,1,0:T(4,128)(2,1)} async-done(((bf16[1024,4,256]{2,1,0:T(4,128)(2,1)}), bf16[1024,4,256]{2,1,0:T(4,128)(2,1)}, u32[]{:S(2)}, u32[]{:S(2)}) %all-to-all-start) | async-done | bytes 2097184 | tf_op jit(solution)/shard_map/all_to_all | solution.py:279
  80.6 4.5 %copy.29 = bf16[4,256,4,256]{3,0,1,2:T(4,128)(2,1)} copy(bf16[4,256,4,256]{3,2,1,0:T(4,128)(2,1)} %bitcast.12) | data formatting | bytes 4194304 | tf_op jit(solution)/shard_map/all_to_all | solution.py:279
  85.1 4.4 %all_to_all.16 = bf16[256,4,1024]{2,0,1:T(8,128)(2,1)} reshape(bf16[256,4,4,256]{3,2,0,1:T(4,128)(2,1)} %bitcast.58) | data formatting | bytes 4194304 | tf_op jit(solution)/shard_map/all_to_all | solution.py:279
  89.5 6.5 %fusion.6 = f32[256,4,1024]{2,0,1:T(8,128)} fusion(bf16[256,4,1024]{2,0,1:T(8,128)(2,1)} %all_to_all.16, bf16[1,1024,1024]{2,1,0:T(8,128)(2,1)} %param.13), kind=kOutput, calls=%fused_computation.9 | convolution fusion | flops 2147483648 | bytes 8388608 | tf_op jit(solution)/shard_map/akc,cy->kay/dot_general | solution.py:277
  96.0 19.5 %all-gather.6.cloned.1.call-done = bf16[1,1024,4,1024]{3,2,0,1:T(4,128)(2,1)} async-done(((bf16[1,256,4,1024]{3,2,0,1:T(4,128)(2,1)}), bf16[1,1024,4,1024]{3,2,0,1:T(4,128)(2,1)}) %all-gather.6.cloned.1.call-update) | async-done | bytes 8388624 | tf_op jit(solution)/shard_map/all_gather | solution.py:265
  115.5 14.7 %reshape.51 = bf16[1024,4096,1]{1,0,2:T(8,128)(2,1)} reshape(bf16[1,1024,4,1024]{3,2,0,1:T(4,128)(2,1)} %all-gather.6.cloned.1.call-done) | data formatting | bytes 16777216 | tf_op jit(solution)/shard_map/reshape | solution.py:269
  130.2 21.2 %fusion.2.projected_ref = f32[6,256,4096]{2,1,0:T(8,128)} fusion(bf16[1024,4096,1]{1,0,2:T(8,128)(2,1)} %reshape.51, bf16[256,6,1024]{2,0,1:T(8,128)(2,1)} %collective-permute-done), kind=kOutput, calls=%fused_computation.4 | convolution fusion | flops 12884901888 | bytes 36700160 | tf_op jit(solution)/shard_map/dot_general | solution.py:267
  151.5 17.9 %mixed.1 = bf16[4,256,6144]{2,1,0:T(8,128)(2,1)S(1)} custom-call(bf16[192,192]{1,0:T(8,128)(2,1)S(1)} %mul.35.spread_ref, f32[6,256,4096]{2,1,0:T(8,128)} %fusion.2.projected_ref), custom_call_target="tpu_custom_call" | custom-call | flops 4831838208 | bytes 37748736 | tf_op jit(solution)/shard_map/mixed/pallas_call | solution.py:242
  169.4 5.9 %copy-done.2 = bf16[4,256,6144]{2,1,0:T(8,128)(2,1)} copy-done((bf16[4,256,6144]{2,1,0:T(8,128)(2,1)}, bf16[4,256,6144]{2,1,0:T(8,128)(2,1)S(1)}, u32[]{:S(2)}) %copy-start.2) | copy-done | bytes 12582936
  175.3 63.9 %all-gather.4.cloned.1.call-done = bf16[6144,1024]{1,0:T(8,128)(2,1)} async-done(((bf16[1536,1024]{1,0:T(8,128)(2,1)}), bf16[6144,1024]{1,0:T(8,128)(2,1)}) %all-gather.4.cloned.1.call-update) | async-done | bytes 12582928 | tf_op jit(solution)/shard_map/all_gather | solution.py:286
  239.2 19.1 %bitcast_subtract_fusion = f32[1024,1024]{1,0:T(8,128)S(1)} fusion(f32[256,4,1024]{2,0,1:T(8,128)} %fusion.6, bf16[1024,6144]{1,0:T(8,128)(2,1)} %bitcast.55, bf16[6144,1024]{1,0:T(8,128)(2,1)} %all-gather.4.cloned.1.call-done), kind=kOutput, calls=%fused_computation | convolution fusion | flops 12886999040 | bytes 33554432 | tf_op jit(solution)/shard_map/dot_general | solution.py:291
  258.3 2.0 fusion.20
  260.3 1.6 fusion
  261.9 1.0 fusion.4
  264.2 59.8 %summed.1 = f32[4,64,2560]{2,1,0:T(8,128)S(1)} custom-call(f32[4,64,2560]{2,1,0:T(8,128)S(1)} %bitcast.56), custom_call_target="tpu_custom_call" | custom-call | tf_op jit(solution)/shard_map/summed/pallas_call | solution.py:96
  324.0 50.2 %factorize.1 = (f32[1024,1024]{1,0:T(8,128)S(1)}, f32[1024,1024]{1,0:T(8,128)S(1)}) custom-call(f32[256,2560]{1,0:T(8,128)S(1)} %bitcast.57), custom_call_target="tpu_custom_call" | custom-call | tf_op jit(solution)/shard_map/factorize/pallas_call | solution.py:192
  374.2 7.0 %multiply_convert_fusion = bf16[1024,1024]{1,0:T(8,128)(2,1)S(1)} fusion(f32[1024,1024]{1,0:T(8,128)S(1)} %bitcast_subtract_fusion, f32[1024,1024]{1,0:T(8,128)S(1)} %get-tuple-element.4), kind=kOutput, calls=%fused_computation.1 | convolution fusion | flops 6444548096 | bytes 10485760 | tf_op jit(solution)/shard_map/dot_general | solution.py:309
  381.2 2.9 copy.28
  384.1 1.1 multiply_bitcast_fusion
  (19 shorter events, 5.0 us)
Async XLA Ops:
  7.2 30.0 %copy-start = (bf16[1,1024,4,256]{3,2,1,0:T(4,128)(2,1)S(1)}, bf16[1,1024,4,256]{3,2,1,0:T(4,128)(2,1)}, u32[]{:S(2)}) copy-start(bf16[1,1024,4,256]{3,2,1,0:T(4,128)(2,1)} %param.10) | copy-start | bytes 6291460
  7.2 108.3 %all-gather.6.cloned.1.call-start = ((), (), s32[]{:S(2)}) async-start(), calls=%async_computation.2 | async-start | bytes 10485760 | tf_op jit(solution)/shard_map/all_gather | solution.py:265
  7.9 231.3 %all-gather.4.cloned.1.call-start = ((), (), s32[]{:S(2)}) async-start(), calls=%async_computation.1 | async-start | bytes 15728640 | tf_op jit(solution)/shard_map/all_gather | solution.py:286
  8.7 28.5 %collective-permute-start.1 = (bf16[1024,1024]{1,0:T(8,128)(2,1)}, bf16[1024,1024]{1,0:T(8,128)(2,1)S(1)}, u32[]{:S(2)}, u32[]{:S(2)}) collective-permute-start(bf16[1024,1024]{1,0:T(8,128)(2,1)} %bitcast.65), channel_id=1, source_target_pairs={{28,0},{0,4},{4,8},{8,12},{12,16},{16,20},{20,24},{24,28},{29,1},{... | collective-permute-start | bytes 6291464 | tf_op jit(solution)/shard_map/ppermute | solution.py:23
  9.2 121.0 %collective-permute-start = (bf16[256,6,1024]{2,0,1:T(8,128)(2,1)}, bf16[256,6,1024]{2,0,1:T(8,128)(2,1)}, u32[]{:S(2)}, u32[]{:S(2)}) collective-permute-start(bf16[256,6,1024]{2,0,1:T(8,128)(2,1)} %bitcast.64), channel_id=1, source_target_pairs={{28,0},{0,4},{4,8},{8,12},{12,16},{16,20},{20,24},{24,28},{29,1},{... | collective-permute-start | bytes 9437192 | tf_op jit(solution)/shard_map/ppermute | solution.py:23
  42.4 4.8 %copy-start.3 = (bf16[1,6,6,4,4]{2,4,3,1,0:T(4,128)(2,1)S(1)}, bf16[1,6,6,4,4]{2,4,3,1,0:T(4,128)(2,1)}, u32[]{:S(2)}) copy-start(bf16[1,6,6,4,4]{2,4,3,1,0:T(4,128)(2,1)} %param.11) | copy-start | bytes 3460
  42.4 38.1 %all-to-all-start = ((bf16[1024,4,256]{2,1,0:T(4,128)(2,1)}), bf16[1024,4,256]{2,1,0:T(4,128)(2,1)}, u32[]{:S(2)}, u32[]{:S(2)}) async-start(bf16[1024,4,256]{2,1,0:T(4,128)(2,1)} %copy.17), calls=%async_computation | async-start | bytes 4194304 | tf_op jit(solution)/shard_map/all_to_all | solution.py:279
  169.3 6.0 %copy-start.2 = (bf16[4,256,6144]{2,1,0:T(8,128)(2,1)}, bf16[4,256,6144]{2,1,0:T(8,128)(2,1)S(1)}, u32[]{:S(2)}) copy-start(bf16[4,256,6144]{2,1,0:T(8,128)(2,1)S(1)} %mixed.1) | copy-start | bytes 37748740
  381.2 4.0 %copy-start.1 = (bf16[1,1024,4,256]{3,2,1,0:T(4,128)(2,1)S(1)}, bf16[1,1024,4,256]{3,2,1,0:T(4,128)(2,1)}, u32[]{:S(2)}) copy-start(bf16[1,1024,4,256]{3,2,1,0:T(4,128)(2,1)} %param.10) | copy-start | bytes 6291460
Sparse Core Ops, SparseCore 0:
  9.8 105.6 all-gather.5
  117.4 121.8 all-gather.3
